TPU v7x, 32 devices: a whole 2x2x4 slice. The times are simulated.
32 devices in a mesh: batch: 2 (over x), seq: 16 (over z, y, core).
Axes of the slice: x: 2, y: 2, z: 4, core: 2. Of those that a mesh axis runs over, the one named last changes fastest.
Arguments:
- inputs: bfloat16 [2, 2048, 1024], P('batch', 'seq'), may hold values from -6 to 6
- seg_ids: int32 [2, 2048], P('batch', 'seq'), may hold values from 0 to 3, never falling along the last dimension, each value on 1 to 1024 neighbouring positions
- gain_attn: bfloat16 [1024], P('batch'), may hold values from 0.5 to 1.5
- w_query: bfloat16 [1024, 512], P('batch'), may hold values from -0.1875 to 0.1875
- w_key: bfloat16 [1024, 512], P('batch'), may hold values from -0.1875 to 0.1875
- w_value: bfloat16 [1024, 1024], P('batch'), may hold values from -0.1875 to 0.1875
- w_outgate: bfloat16 [1024, 1024], P('batch'), may hold values from -0.1875 to 0.1875
- w_rank_in: bfloat16 [1024, 16], P('batch'), may hold values from -0.1875 to 0.1875
- w_rank_out: bfloat16 [16, 512], P(None, 'batch'), may hold values from -1.5 to 1.5
- rank_bias: bfloat16 [512], P('batch'), may hold values from -0.5 to 6
- head_gain: bfloat16 [256], P('batch'), may hold values from 0.5 to 1.5
- w_output: bfloat16 [1024, 1024], P(None, 'batch'), may hold values from -0.1875 to 0.1875
- gain_ffn: bfloat16 [1024], P('batch'), may hold values from 0.5 to 1.5
- w_gate: bfloat16 [1024, 2816], P('batch'), may hold values from -0.1875 to 0.1875
- w_up: bfloat16 [1024, 2816], P('batch'), may hold values from -0.1875 to 0.1875
- w_down: bfloat16 [2816, 1024], P('batch'), may hold values from -0.109375 to 0.109375
- cotangent: bfloat16 [2, 2048, 1024], P('batch', 'seq'), may hold values from -6 to 6
Outputs:
- output: bfloat16 [2, 2048, 1024], P('batch', 'seq')
- grad_inputs: bfloat16 [2, 2048, 1024], P('batch', 'seq')
- grad_gain_attn: float32 [1024], P('batch')
- grad_w_query: float32 [1024, 512], P('batch')
- grad_w_key: float32 [1024, 512], P('batch')
- grad_w_value: float32 [1024, 1024], P('batch')
- grad_w_outgate: float32 [1024, 1024], P('batch')
- grad_w_rank_in: float32 [1024, 16], P('batch')
- grad_w_rank_out: float32 [16, 512], P(None, 'batch')
- grad_rank_bias: float32 [512], P('batch')
- grad_head_gain: float32 [256], P('batch')
- grad_w_output: float32 [1024, 1024], P(None, 'batch')
- grad_gain_ffn: float32 [1024], P('batch')
- grad_w_gate: float32 [1024, 2816], P('batch')
- grad_w_up: float32 [1024, 2816], P('batch')
- grad_w_down: float32 [2816, 1024], P('batch')
Inputs may be any that keep to these rules, and one draw needn't show every extreme that they name: `seg_ids`: along each sequence document ids never fall; each document holds 1 to 1024 tokens and one holds exactly 1024.
All inputs are finite; a program needn't handle non-finite values.
Results may differ from a plain program's by a relative error of at most 0.023.
Values may be sent and summed in bfloat16 or wider, within the bound.
A program may use at most 192 MiB of HBM per device.

v0:
```python
import jax
import jax.numpy as jnp
from jax import lax
from jax.sharding import PartitionSpec as P

HEADS = 4
DK = 128
DV = 256
SPAN = 64
KEYS = 512
VALS = 1024


norm_eps = 1e-05
head_eps = 0.1
top_prec = lax.Precision.HIGHEST


def prefix_2(value, axis, join, neutral):
    place = lax.axis_index(axis)
    gathered = jax.tree.map(
        lambda a, kind: lax.all_gather(a.astype(kind), axis),
        value,
        (jnp.bfloat16, jnp.bfloat16, jnp.bfloat16, jnp.bfloat16),
    )
    state = jax.tree.map(lambda a, e: jnp.zeros_like(a) + jnp.asarray(e, a.dtype), value, neutral)

    def one(turn, state):
        return join(
            state,
            jax.tree.map(
                lambda a, own: lax.dynamic_index_in_dim(a, turn, 0, False).astype(own.dtype),
                gathered,
                value,
            ),
        )

    return lax.fori_loop(0, place, one, state)


def entering(value, axis, combine, identity):
    peers, mine = (lax.axis_size(axis), lax.axis_index(axis))
    everything = jax.tree.map(
        lambda part, kind: lax.all_gather(part.astype(kind), axis),
        value,
        jax.tree.map(lambda a: jnp.bfloat16 if a.dtype == jnp.float32 else a.dtype, value),
    )
    start = jax.tree.map(
        lambda part, zero: jnp.broadcast_to(jnp.asarray(zero, part.dtype), part.shape),
        value,
        identity,
    )

    def turn(k, before):
        at = peers - 1 - k
        reached = at > mine
        new = combine(
            before, jax.tree.map(lambda part, own: part[at].astype(own.dtype), everything, value)
        )
        return jax.tree.map(lambda a, b: jnp.where(reached, a, b), new, before)

    return lax.fori_loop(0, peers, turn, start)


def rms_scale(values_in):
    return lax.rsqrt(jnp.mean(values_in * values_in, axis=-1, keepdims=True) + norm_eps)


def head_rms(values_in):
    return lax.rsqrt(jnp.mean(values_in * values_in, axis=-1, keepdims=True) + head_eps)


def span_step(carried_in, inputs_now):
    state_now, prior_id = carried_in
    queries, key_rows, value_rows, decays, seg_now = inputs_now
    span_len = queries.shape[0]
    cumulative = jnp.cumsum(decays, axis=0)
    first_id = seg_now[0]
    state_now = state_now * (prior_id == first_id).astype(jnp.float32)
    within_doc = (seg_now == first_id).astype(jnp.float32)
    query_dec = queries * jnp.exp(cumulative)
    key_dec = key_rows * jnp.exp(-cumulative)
    scores = jnp.einsum("thc,shc->hts", query_dec, key_dec, precision=top_prec)
    row_pos = lax.broadcasted_iota(jnp.int32, (span_len, span_len), 0)
    col_pos = lax.broadcasted_iota(jnp.int32, (span_len, span_len), 1)
    allowed = jnp.logical_and(col_pos <= row_pos, seg_now[:, None] == seg_now[None, :]).astype(
        jnp.float32
    )
    scores = scores * allowed[None]
    span_out = jnp.einsum("hts,shv->thv", scores, value_rows, precision=top_prec)
    span_out = span_out + within_doc[:, None, None] * jnp.einsum(
        "thc,hcv->thv", query_dec, state_now, precision=top_prec
    )
    last_cumul = cumulative[-1]
    end_doc = (seg_now == seg_now[-1]).astype(jnp.float32)
    key_end = key_rows * jnp.exp(last_cumul[None] - cumulative) * end_doc[:, None, None]
    next_state = (jnp.exp(last_cumul) * within_doc[-1])[:, :, None] * state_now
    next_state = next_state + jnp.einsum("shc,shv->hcv", key_end, value_rows, precision=top_prec)
    return ((next_state, seg_now[-1]), span_out)


def gla_run(queries, key_rows, value_rows, decays, seg_row, start_state, prior_id):
    tok_count = queries.shape[0]
    num_spans = tok_count // SPAN

    def blocks(array_in):
        return array_in.reshape((num_spans, SPAN) + array_in.shape[1:])

    (final_state, last_id), outs_all = lax.scan(
        span_step,
        (start_state, prior_id),
        (
            blocks(queries),
            blocks(key_rows),
            blocks(value_rows),
            blocks(decays),
            seg_row.reshape(num_spans, SPAN),
        ),
    )
    return (outs_all.reshape((tok_count,) + outs_all.shape[2:]), final_state)


def silu_grad(pre_act, sig_val):
    return sig_val * (1.0 + pre_act * (1.0 - sig_val))


def combine_forward(earlier, later):
    decay_early, state_early, first_early, last_early = earlier
    decay_late, state_late, first_late, last_late = later
    linked = jnp.logical_or(
        last_early == first_late, jnp.logical_or(last_early < 0.0, first_late < 0.0)
    ).astype(jnp.float32)
    carry_factor = decay_late * linked
    return (
        decay_early * carry_factor,
        carry_factor[:, :, None] * state_early + state_late,
        jnp.where(first_early < 0.0, first_late, first_early),
        jnp.where(last_late < 0.0, last_early, last_late),
    )


def combine_backward(earlier, later):
    decay_early, grad_early, first_early, last_early = earlier
    decay_late, grad_late, first_late, last_late = later
    linked = jnp.logical_or(
        last_late == first_early, jnp.logical_or(last_late < 0.0, first_early < 0.0)
    ).astype(jnp.float32)
    carry_factor = decay_late * linked
    return (
        carry_factor * decay_early,
        grad_late + carry_factor[:, :, None] * grad_early,
        jnp.where(first_late < 0.0, first_early, first_late),
        jnp.where(last_early < 0.0, last_late, last_early),
    )


def per_device(
    inputs,
    seg_ids,
    gain_attn,
    w_query,
    w_key,
    w_value,
    w_outgate,
    w_rank_in,
    w_rank_out,
    rank_bias,
    head_gain,
    w_output,
    gain_ffn,
    w_gate,
    w_up,
    w_down,
    cotangent,
):
    f32 = jnp.float32
    bf16 = jnp.bfloat16
    (
        gain_one,
        query_w,
        key_w,
        value_w,
        outgate_w,
        rank_in_w,
        rank_out_w,
        bias_w,
        headgain_w,
        output_w,
        gain_two,
        gate_w,
        up_w,
        down_w,
    ) = (
        lax.all_gather(gain_attn, "batch", axis=0, tiled=True),
        lax.all_gather(w_query, "batch", axis=0, tiled=True),
        lax.all_gather(w_key, "batch", axis=0, tiled=True),
        lax.all_gather(w_value, "batch", axis=0, tiled=True),
        lax.all_gather(w_outgate, "batch", axis=0, tiled=True),
        lax.all_gather(w_rank_in, "batch", axis=0, tiled=True),
        lax.all_gather(w_rank_out, "batch", axis=1, tiled=True),
        lax.all_gather(rank_bias, "batch", axis=0, tiled=True),
        lax.all_gather(head_gain, "batch", axis=0, tiled=True),
        lax.all_gather(w_output, "batch", axis=1, tiled=True),
        lax.all_gather(gain_ffn, "batch", axis=0, tiled=True),
        lax.all_gather(w_gate, "batch", axis=0, tiled=True),
        lax.all_gather(w_up, "batch", axis=0, tiled=True),
        lax.all_gather(w_down, "batch", axis=0, tiled=True),
    )
    activation = inputs[0].astype(f32)
    seg_row = seg_ids[0]
    tok_count = activation.shape[0]
    scale_one = rms_scale(activation)
    unit_one = activation * scale_one
    normed = (unit_one * gain_one.astype(f32)).astype(bf16)
    queries = jnp.dot(normed, query_w, preferred_element_type=f32) * DK ** (-0.5)
    keys_all = jnp.dot(normed, key_w, preferred_element_type=f32)
    values_all = jnp.dot(normed, value_w, preferred_element_type=f32)
    outgate = jnp.dot(normed, outgate_w, preferred_element_type=f32)
    low_rank = jnp.dot(normed, rank_in_w, preferred_element_type=f32)
    logits = jnp.dot(low_rank, rank_out_w.astype(f32), precision=top_prec) + bias_w.astype(f32)
    decays = jax.nn.log_sigmoid(logits) / 16.0
    queries_h = queries.reshape(tok_count, HEADS, DK)
    keys_h = keys_all.reshape(tok_count, HEADS, DK)
    values_h = values_all.reshape(tok_count, HEADS, DV)
    decays_h = decays.reshape(tok_count, HEADS, DK)
    local_out, local_state = gla_run(
        queries_h,
        keys_h,
        values_h,
        decays_h,
        seg_row,
        jnp.zeros((HEADS, DK, DV), f32),
        jnp.int32(-1),
    )
    cumulative = jnp.cumsum(decays_h, axis=0)
    same_first = (seg_row == seg_row[0]).astype(f32)
    first_id = seg_row[0].astype(f32)
    last_id = seg_row[-1].astype(f32)
    block_decay = jnp.exp(cumulative[-1]) * same_first[-1]
    start_ident = (
        jnp.ones_like(block_decay),
        jnp.zeros_like(local_state),
        jnp.float32(-1.0),
        jnp.float32(-1.0),
    )
    prefix = prefix_2(
        (block_decay, local_state, first_id, last_id), "seq", combine_forward, start_ident
    )
    linked_in = jnp.logical_or(prefix[3] == first_id, prefix[3] < 0.0).astype(f32)
    carried = prefix[1] * linked_in
    reach_q = queries_h * jnp.exp(cumulative) * same_first[:, None, None]
    attn_raw = local_out + jnp.einsum("thc,hcv->thv", reach_q, carried, precision=top_prec)
    head_scale = head_rms(attn_raw)
    head_norm = attn_raw * head_scale
    gate_h = outgate.reshape(tok_count, HEADS, DV)
    gate_sig = jax.nn.sigmoid(gate_h)
    gate_act = gate_h * gate_sig
    head_gain32 = headgain_w.astype(f32)
    gated = (head_norm * head_gain32 * gate_act).reshape(tok_count, VALS).astype(bf16)
    resid = activation + jnp.dot(gated, output_w, preferred_element_type=f32)
    scale_two = rms_scale(resid)
    unit_two = resid * scale_two
    normed_two = (unit_two * gain_two.astype(f32)).astype(bf16)
    gate_pre = jnp.dot(normed_two, gate_w, preferred_element_type=f32)
    up_pre = jnp.dot(normed_two, up_w, preferred_element_type=f32)
    ffn_sig = jax.nn.sigmoid(gate_pre)
    hidden = (gate_pre * ffn_sig * up_pre).astype(bf16)
    output = (resid + jnp.dot(hidden, down_w, preferred_element_type=f32)).astype(bf16)
    (
        gain_one,
        query_w,
        key_w,
        value_w,
        outgate_w,
        rank_in_w,
        rank_out_w,
        bias_w,
        headgain_w,
        output_w,
        gain_two,
        gate_w,
        up_w,
        down_w,
    ) = (
        lax.all_gather(gain_attn, "batch", axis=0, tiled=True),
        lax.all_gather(w_query, "batch", axis=0, tiled=True),
        lax.all_gather(w_key, "batch", axis=0, tiled=True),
        lax.all_gather(w_value, "batch", axis=0, tiled=True),
        lax.all_gather(w_outgate, "batch", axis=0, tiled=True),
        lax.all_gather(w_rank_in, "batch", axis=0, tiled=True),
        lax.all_gather(w_rank_out, "batch", axis=1, tiled=True),
        lax.all_gather(rank_bias, "batch", axis=0, tiled=True),
        lax.all_gather(head_gain, "batch", axis=0, tiled=True),
        lax.all_gather(w_output, "batch", axis=1, tiled=True),
        lax.all_gather(gain_ffn, "batch", axis=0, tiled=True),
        lax.all_gather(w_gate, "batch", axis=0, tiled=True),
        lax.all_gather(w_up, "batch", axis=0, tiled=True),
        lax.all_gather(w_down, "batch", axis=0, tiled=True),
    )
    cot_rows = cotangent[0]
    grad_down = jnp.dot(hidden.T, cot_rows, preferred_element_type=f32)
    grad_hidden = jnp.dot(cot_rows, down_w.T, preferred_element_type=f32)
    grad_gate_pre = (grad_hidden * up_pre * silu_grad(gate_pre, ffn_sig)).astype(bf16)
    grad_up_pre = (grad_hidden * gate_pre * ffn_sig).astype(bf16)
    grad_gate = jnp.dot(normed_two.T, grad_gate_pre, preferred_element_type=f32)
    grad_up = jnp.dot(normed_two.T, grad_up_pre, preferred_element_type=f32)
    grad_normed_two = jnp.dot(grad_gate_pre, gate_w.T, preferred_element_type=f32) + jnp.dot(
        grad_up_pre, up_w.T, preferred_element_type=f32
    )
    grad_gain_two = jnp.sum(grad_normed_two * unit_two, axis=0)
    scaled_two = grad_normed_two * gain_two.astype(f32)
    grad_resid = cot_rows.astype(f32) + scale_two * (
        scaled_two - unit_two * jnp.mean(scaled_two * unit_two, axis=-1, keepdims=True)
    )
    resid_bf = grad_resid.astype(bf16)
    grad_output = jnp.dot(gated.T, resid_bf, preferred_element_type=f32)
    grad_gated = jnp.dot(resid_bf, output_w.T, preferred_element_type=f32).reshape(
        tok_count, HEADS, DV
    )
    grad_headgain = jnp.sum(grad_gated * head_norm * gate_act, axis=(0, 1))
    grad_gate_h = grad_gated * head_norm * head_gain32 * silu_grad(gate_h, gate_sig)
    grad_norm_h = grad_gated * head_gain32 * gate_act
    grad_attn = head_scale * (
        grad_norm_h - head_norm * jnp.mean(grad_norm_h * head_norm, axis=-1, keepdims=True)
    )
    reach_grad = jnp.einsum("thc,thv->hcv", reach_q, grad_attn, precision=top_prec)
    end_ident = (
        jnp.ones_like(block_decay),
        jnp.zeros_like(reach_grad),
        jnp.float32(-1.0),
        jnp.float32(-1.0),
    )
    suffix = entering(
        (block_decay, reach_grad, first_id, last_id), "seq", combine_backward, end_ident
    )
    linked_out = jnp.logical_or(suffix[2] == last_id, suffix[2] < 0.0).astype(f32)
    grad_end = suffix[1] * linked_out

    def carried_run(queries_in, keys_in, values_in, decays_in):
        return gla_run(queries_in, keys_in, values_in, decays_in, seg_row, carried, seg_row[0])

    run_out, pullback = jax.vjp(carried_run, queries_h, keys_h, values_h, decays_h)
    grad_q, grad_k, grad_v, grad_d = pullback((grad_attn, grad_end))
    grad_logits = grad_d.reshape(tok_count, KEYS) * jax.nn.sigmoid(-logits) / 16.0
    grad_bias = jnp.sum(grad_logits, axis=0)
    grad_rank_out = jnp.dot(low_rank.T, grad_logits, precision=top_prec)
    grad_low = jnp.dot(grad_logits, rank_out_w.astype(f32).T, precision=top_prec).astype(bf16)
    query_grad = (grad_q.reshape(tok_count, KEYS) * DK ** (-0.5)).astype(bf16)
    key_grad = grad_k.reshape(tok_count, KEYS).astype(bf16)
    value_grad = grad_v.reshape(tok_count, VALS).astype(bf16)
    outgate_grad = grad_gate_h.reshape(tok_count, VALS).astype(bf16)
    grad_normed = (
        jnp.dot(query_grad, query_w.T, preferred_element_type=f32)
        + jnp.dot(key_grad, key_w.T, preferred_element_type=f32)
        + jnp.dot(value_grad, value_w.T, preferred_element_type=f32)
        + jnp.dot(outgate_grad, outgate_w.T, preferred_element_type=f32)
        + jnp.dot(grad_low, rank_in_w.T, preferred_element_type=f32)
    )
    grad_gain_one = jnp.sum(grad_normed * unit_one, axis=0)
    scaled_one = grad_normed * gain_one.astype(f32)
    grad_input = (
        grad_resid
        + scale_one
        * (scaled_one - unit_one * jnp.mean(scaled_one * unit_one, axis=-1, keepdims=True))
    ).astype(bf16)
    grad_query = jnp.dot(normed.T, query_grad, preferred_element_type=f32)
    grad_key = jnp.dot(normed.T, key_grad, preferred_element_type=f32)
    grad_value = jnp.dot(normed.T, value_grad, preferred_element_type=f32)
    grad_outgate = jnp.dot(normed.T, outgate_grad, preferred_element_type=f32)
    grad_rank_in = jnp.dot(normed.T, grad_low, preferred_element_type=f32)
    owned = (
        lax.psum_scatter(
            grad_gain_one.astype(jnp.bfloat16), "batch", scatter_dimension=0, tiled=True
        ).astype(jnp.float32),
        lax.psum_scatter(
            grad_query.astype(jnp.bfloat16), "batch", scatter_dimension=0, tiled=True
        ).astype(jnp.float32),
        lax.psum_scatter(
            grad_key.astype(jnp.bfloat16), "batch", scatter_dimension=0, tiled=True
        ).astype(jnp.float32),
        lax.psum_scatter(
            grad_value.astype(jnp.bfloat16), "batch", scatter_dimension=0, tiled=True
        ).astype(jnp.float32),
        lax.psum_scatter(
            grad_outgate.astype(jnp.bfloat16), "batch", scatter_dimension=0, tiled=True
        ).astype(jnp.float32),
        lax.psum_scatter(
            grad_rank_in.astype(jnp.bfloat16), "batch", scatter_dimension=0, tiled=True
        ).astype(jnp.float32),
        lax.psum_scatter(
            grad_rank_out.astype(jnp.bfloat16), "batch", scatter_dimension=1, tiled=True
        ).astype(jnp.float32),
        lax.psum_scatter(
            grad_bias.astype(jnp.bfloat16), "batch", scatter_dimension=0, tiled=True
        ).astype(jnp.float32),
        lax.psum_scatter(
            grad_headgain.astype(jnp.bfloat16), "batch", scatter_dimension=0, tiled=True
        ).astype(jnp.float32),
        lax.psum_scatter(
            grad_output.astype(jnp.bfloat16), "batch", scatter_dimension=1, tiled=True
        ).astype(jnp.float32),
        lax.psum_scatter(
            grad_gain_two.astype(jnp.bfloat16), "batch", scatter_dimension=0, tiled=True
        ).astype(jnp.float32),
        lax.psum_scatter(
            grad_gate.astype(jnp.bfloat16), "batch", scatter_dimension=0, tiled=True
        ).astype(jnp.float32),
        lax.psum_scatter(
            grad_up.astype(jnp.bfloat16), "batch", scatter_dimension=0, tiled=True
        ).astype(jnp.float32),
        lax.psum_scatter(
            grad_down.astype(jnp.bfloat16), "batch", scatter_dimension=0, tiled=True
        ).astype(jnp.float32),
    )
    summed = (
        lax.psum(owned[0].astype(jnp.bfloat16), "seq").astype(jnp.float32),
        lax.psum(owned[1].astype(jnp.bfloat16), "seq").astype(jnp.float32),
        lax.psum(owned[2].astype(jnp.bfloat16), "seq").astype(jnp.float32),
        lax.psum(owned[3].astype(jnp.bfloat16), "seq").astype(jnp.float32),
        lax.psum(owned[4].astype(jnp.bfloat16), "seq").astype(jnp.float32),
        lax.psum(owned[5].astype(jnp.bfloat16), "seq").astype(jnp.float32),
        lax.psum(owned[6].astype(jnp.bfloat16), "seq").astype(jnp.float32),
        lax.psum(owned[7].astype(jnp.bfloat16), "seq").astype(jnp.float32),
        lax.psum(owned[8].astype(jnp.bfloat16), "seq").astype(jnp.float32),
        lax.psum(owned[9].astype(jnp.bfloat16), "seq").astype(jnp.float32),
        lax.psum(owned[10].astype(jnp.bfloat16), "seq").astype(jnp.float32),
        lax.psum(owned[11].astype(jnp.bfloat16), "seq").astype(jnp.float32),
        lax.psum(owned[12].astype(jnp.bfloat16), "seq").astype(jnp.float32),
        lax.psum(owned[13].astype(jnp.bfloat16), "seq").astype(jnp.float32),
    )
    return (
        output[None],
        grad_input[None],
        summed[0],
        summed[1],
        summed[2],
        summed[3],
        summed[4],
        summed[5],
        summed[6],
        summed[7],
        summed[8],
        summed[9],
        summed[10],
        summed[11],
        summed[12],
        summed[13],
    )


def solution(mesh):
    in_specs = (
        P("batch", "seq", None),
        P("batch", "seq"),
        P("batch"),
        P("batch", None),
        P("batch", None),
        P("batch", None),
        P("batch", None),
        P("batch", None),
        P(None, "batch"),
        P("batch"),
        P("batch"),
        P(None, "batch"),
        P("batch"),
        P("batch", None),
        P("batch", None),
        P("batch", None),
        P("batch", "seq", None),
    )
    out_specs = (
        P("batch", "seq", None),
        P("batch", "seq", None),
        P("batch"),
        P("batch", None),
        P("batch", None),
        P("batch", None),
        P("batch", None),
        P("batch", None),
        P(None, "batch"),
        P("batch"),
        P("batch"),
        P(None, "batch"),
        P("batch"),
        P("batch", None),
        P("batch", None),
        P("batch", None),
    )
    return jax.shard_map(
        per_device, mesh=mesh, in_specs=in_specs, out_specs=out_specs, check_vma=False
    )
```

profile of v0, /device:TPU:0, one launch (start us, length us, event | category | flops | bytes accessed | tf_op | source)
XLA Modules:
  0.0 1221.5 jit_solution(8478155007797639958)
XLA Ops:
  10.1 5.2 all-gather.3
  36.0 20.7 %all-gather.21.cloned.1.call-done = bf16[1024,512]{1,0:T(8,128)(2,1)} async-done(((bf16[512,512]{1,0:T(8,128)(2,1)}), bf16[1024,512]{1,0:T(8,128)(2,1)}) %all-gather.21.cloned.1.call-update) | async-done | bytes 1048592 | tf_op jit(solution)/shard_map/all_gather | solution.py:195
  58.4 33.0 %all-gather.19.cloned.1.call-done = bf16[1024,1024]{1,0:T(8,128)(2,1)} async-done(((bf16[512,1024]{1,0:T(8,128)(2,1)}), bf16[1024,1024]{1,0:T(8,128)(2,1)}) %all-gather.19.cloned.1.call-update) | async-done | bytes 2097168 | tf_op jit(solution)/shard_map/all_gather | solution.py:197
  97.7 17.0 %while.117 = (s32[]{:T(128)}, f32[4,128,256]{2,1,0:T(8,128)S(1)}, s32[]{:T(128)}, f32[2,64,4,256]{3,1,0,2:T(8,128)}, f32[2,64,4,128]{3,2,1,0:T(4,128)}, /*index=...) while((s32[]{:T(128)}, f32[4,128,256]{2,1,0:T(8,128)S(1)}, ...), condition=%wide.region_3.4_spmd.clone, body=%wide.region_1.3_spmd.clone.sunk | while | flops 280036096 | bytes 8896274 | solution.py:109
  122.3 33.3 %all-reduce.8 = (bf16[16]{0:T(256)(128)(2,1)S(1)}, bf16[16]{0:T(256)(128)(2,1)S(1)}) all-reduce(bf16[16]{0:T(256)(128)(2,1)S(1)} %dynamic-update-slice, bf16[16]{0:T(256)(128)(2,1)S(1)} %dynamic-update-slice.1), channel_id=1, replica_groups=mesh['batch'=2,'seq'=16] {'seq'}, use_global_device_ids=true, to_apply=%add.1 | all-reduce | flops 32 | bytes 128
  166.2 17.3 %all_gather.95 = bf16[16,4,128]{2,1,0:T(4,128)(2,1)S(1)} all-gather(bf16[1,4,128]{2,1,0:T(4,128)(2,1)S(1)} %fusion.145), channel_id=1, replica_groups=mesh['batch'=2,'seq'=16] {'seq'}, dimensions={0}, use_global_device_ids=true | all-gather | bytes 17408 | tf_op jit(solution)/shard_map/all_gather | solution.py:22
  192.2 19.9 %all-gather.25.cloned.1.call-done = bf16[1024,1024]{1,0:T(8,128)(2,1)} async-done(((bf16[1024,512]{1,0:T(8,128)(2,1)}), bf16[1024,1024]{1,0:T(8,128)(2,1)}) %all-gather.25.cloned.1.call-update) | async-done | bytes 2097168 | tf_op jit(solution)/shard_map/all_gather | solution.py:203
  214.4 73.8 %all-gather.27.cloned.1.call-done = bf16[1024,2816]{1,0:T(8,128)(2,1)} async-done(((bf16[512,2816]{1,0:T(8,128)(2,1)}), bf16[1024,2816]{1,0:T(8,128)(2,1)}) %all-gather.27.cloned.1.call-update) | async-done | bytes 5767184 | tf_op jit(solution)/shard_map/all_gather | solution.py:205
  292.9 71.3 %all-gather.29.cloned.1.call-done = bf16[1024,2816]{1,0:T(8,128)(2,1)} async-done(((bf16[512,2816]{1,0:T(8,128)(2,1)}), bf16[1024,2816]{1,0:T(8,128)(2,1)}) %all-gather.29.cloned.1.call-update) | async-done | bytes 5767184 | tf_op jit(solution)/shard_map/all_gather | solution.py:206
  368.9 71.4 %all-gather.31.cloned.1.call-done = bf16[2816,1024]{1,0:T(8,128)(2,1)} async-done(((bf16[1408,1024]{1,0:T(8,128)(2,1)}), bf16[2816,1024]{1,0:T(8,128)(2,1)}) %all-gather.31.cloned.1.call-update) | async-done | bytes 5767184 | tf_op jit(solution)/shard_map/all_gather | solution.py:207
  440.2 6.6 multiply_convert_fusion
  446.8 5.2 fusion.160
  472.2 30.1 %while.116 = (s32[]{:T(128)}, f32[4,128,256]{2,1,0:T(8,128)S(1)}, s32[]{:T(128)}, f32[2]{0:T(128)}, f32[2,64,4,128]{3,2,1,0:T(4,128)}, /*index=5*/f32[2,64,4,128...) while((s32[]{:T(128)}, f32[4,128,256]{2,1,0:T(8,128)S(1)}, ...), condition=%wide.region_15.16_spmd.clone.clone, body=%wide.region_13.15_spmd.clone.clone.sunk | while | flops 128861632 | bytes 5205188 | solution.py:109
  502.3 7.5 all-gather.35.cloned.1.call-done
  509.8 90.6 %while.118 = (s32[]{:T(128)}, f32[4,128,256]{2,1,0:T(8,128)S(1)}, f32[]{:T(128)}, s32[]{:T(128)}, bf16[16,4,128,256]{3,2,1,0:T(8,128)(2,1)}, /*index=5*/bf16[16,...) while((s32[]{:T(128)}, f32[4,128,256]{2,1,0:T(8,128)S(1)}, ...), condition=%wide.region_12.13_spmd.clone, body=%wide.region_11.12_spmd.clone.sunk | while | flops 656401 | bytes 1316132 | solution.py:62
  602.7 20.0 %while.115 = (s32[]{:T(128)}, f32[4,128,256]{2,1,0:T(8,128)S(1)}, f32[2,64,4,128]{3,1,2,0:T(8,128)}, bf16[2,64,4,128]{3,1,2,0:T(8,128)(2,1)}, bf16[2,64,4,256]{3...) while((s32[]{:T(128)}, f32[4,128,256]{2,1,0:T(8,128)S(1)}, ...), condition=%wide.region_20.21_spmd, body=%wide.region_16.20_spmd.sunk | while | flops 557236736 | bytes 26319264 | solution.py:109
  649.5 18.7 %reduce-scatter.13.cloned.1.call-done = bf16[512,512]{1,0:T(8,128)(2,1)} async-done(((bf16[1024,512]{1,0:T(8,128)(2,1)}), bf16[512,512]{1,0:T(8,128)(2,1)}) %reduce-scatter.13.cloned.1.call-update) | async-done | bytes 524304 | tf_op jit(solution)/shard_map/reduce_scatter | solution.py:378
  668.2 74.2 %reduce-scatter.25.cloned.1.call-done = bf16[512,2816]{1,0:T(8,128)(2,1)} async-done(((bf16[1024,2816]{1,0:T(8,128)(2,1)}), bf16[512,2816]{1,0:T(8,128)(2,1)}) %reduce-scatter.25.cloned.1.call-update) | async-done | bytes 2883600 | tf_op jit(solution)/shard_map/reduce_scatter | solution.py:405
  742.4 74.2 %reduce-scatter.27.cloned.1.call-done = bf16[512,2816]{1,0:T(8,128)(2,1)} async-done(((bf16[1024,2816]{1,0:T(8,128)(2,1)}), bf16[512,2816]{1,0:T(8,128)(2,1)}) %reduce-scatter.27.cloned.1.call-update) | async-done | bytes 2883600 | tf_op jit(solution)/shard_map/reduce_scatter | solution.py:408
  816.6 74.2 %reduce-scatter.29.cloned.1.call-done = bf16[1408,1024]{1,0:T(8,128)(2,1)} async-done(((bf16[2816,1024]{1,0:T(8,128)(2,1)}), bf16[1408,1024]{1,0:T(8,128)(2,1)}) %reduce-scatter.29.cloned.1.call-update) | async-done | bytes 2883600 | tf_op jit(solution)/shard_map/reduce_scatter | solution.py:411
  890.8 34.6 %reduce-scatter.15.cloned.1.call-done = bf16[512,1024]{1,0:T(8,128)(2,1)} async-done(((bf16[1024,1024]{1,0:T(8,128)(2,1)}), bf16[512,1024]{1,0:T(8,128)(2,1)}) %reduce-scatter.15.cloned.1.call-update) | async-done | bytes 1048592 | tf_op jit(solution)/shard_map/reduce_scatter | solution.py:381
  942.9 7.3 reduce-scatter.19.cloned.1.call-done
  950.2 63.5 %all-reduce.7 = (bf16[512]{0:T(512)(128)(2,1)S(1)}, bf16[512,16]{0,1:T(8,128)(2,1)S(1)}, bf16[16,256]{1,0:T(8,128)(2,1)S(1)}, bf16[256]{0:T(256)(128)(2,1)S(1)},...) all-reduce(bf16[512]{0:T(512)(128)(2,1)S(1)} %dynamic-slice.3, ...), channel_id=1, replica_groups=mesh['batch'=2,'seq'=16] {'seq'}, use_global_device_ids=true, to_apply=%region_24.25 | all-reduce | flops 13696 | bytes 54784 | tf_op jit(solution)/shard_map/psum | solution.py:416
  1017.2 177.7 %all-reduce.13.cloned.1.call-done = (bf16[512,512]{1,0:T(8,128)(2,1)}, bf16[512,512]{1,0:T(8,128)(2,1)}, bf16[512,1024]{1,0:T(8,128)(2,1)}, bf16[512,1024]{1,0:T...) async-done(((bf16[512,512]{1,0:T(8,128)(2,1)}, bf16[512,512]{1,0:T(8,128)(2,1)}, ...) | async-done | bytes 12845072 | tf_op jit(solution)/shard_map/psum | solution.py:417
  (601 shorter events, 264.5 us)
Async XLA Ops:
  7.2 26.6 %all-gather.17.cloned.1.call-start = ((), (), s32[]{:S(2)}) async-start(), calls=%async_computation.10 | async-start | bytes 1572864 | tf_op jit(solution)/shard_map/all_gather | solution.py:196
  8.0 48.7 %all-gather.21.cloned.1.call-start = ((), (), s32[]{:S(2)}) async-start(), calls=%async_computation.12 | async-start | bytes 1572864 | tf_op jit(solution)/shard_map/all_gather | solution.py:195
  8.7 82.6 %all-gather.19.cloned.1.call-start = ((), (), s32[]{:S(2)}) async-start(), calls=%async_computation.11 | async-start | bytes 3145728 | tf_op jit(solution)/shard_map/all_gather | solution.py:197
  9.5 175.3 %all-gather.23.cloned.1.call-start = ((), (), s32[]{:S(2)}) async-start(), calls=%async_computation.13 | async-start | bytes 3145728 | tf_op jit(solution)/shard_map/all_gather | solution.py:198
  10.0 178.8 %all-gather.33.cloned.1.call-start = ((), (), s32[]{:S(2)}) async-start(), calls=%async_computation.28 | async-start | bytes 4456448 | tf_op jit(solution)/shard_map/all_gather | solution.py:22
  24.5 436.8 %copy-start.8 = (bf16[1,128,1024]{2,1,0:T(8,128)(2,1)}, bf16[1,128,1024]{2,1,0:T(8,128)(2,1)S(1)}, u32[]{:S(2)}) copy-start(bf16[1,128,1024]{2,1,0:T(8,128)(2,1)S(1)} %fusion.117) | copy-start | bytes 786436
  115.5 96.7 %all-gather.25.cloned.1.call-start = ((), (), s32[]{:S(2)}) async-start(), calls=%async_computation.14 | async-start | bytes 3145728 | tf_op jit(solution)/shard_map/all_gather | solution.py:203
  116.1 172.1 %all-gather.27.cloned.1.call-start = ((), (), s32[]{:S(2)}) async-start(), calls=%async_computation.15 | async-start | bytes 8650752 | tf_op jit(solution)/shard_map/all_gather | solution.py:205
  116.8 247.4 %all-gather.29.cloned.1.call-start = ((), (), s32[]{:S(2)}) async-start(), calls=%async_computation.16 | async-start | bytes 8650752 | tf_op jit(solution)/shard_map/all_gather | solution.py:206
  117.6 322.6 %all-gather.31.cloned.1.call-start = ((), (), s32[]{:S(2)}) async-start(), calls=%async_computation.17 | async-start | bytes 8650752 | tf_op jit(solution)/shard_map/all_gather | solution.py:207
  118.3 391.5 %all-gather.35.cloned.1.call-start = ((), (), s32[]{:S(2)}) async-start(), calls=%async_computation.29 | async-start | bytes 4456448 | tf_op jit(solution)/shard_map/all_gather | solution.py:44
  214.3 240.4 %copy-start.4 = (f32[128,1024]{1,0:T(8,128)}, f32[128,1024]{1,0:T(8,128)S(1)}, u32[]{:S(2)}) copy-start(f32[128,1024]{1,0:T(8,128)S(1)} %get-tuple-element.1537) | copy-start | bytes 1572868
  214.4 149.8 %copy-start.2 = (bf16[128,1024]{1,0:T(8,128)(2,1)}, bf16[128,1024]{1,0:T(8,128)(2,1)S(1)}, u32[]{:S(2)}) copy-start(bf16[128,1024]{1,0:T(8,128)(2,1)S(1)} %multiply_convert_fusion.4) | copy-start | bytes 786436
  459.3 190.2 %reduce-scatter.17.cloned.1.call-start = ((), (), s32[]{:S(2)}) async-start(), calls=%async_computation.21 | async-start | bytes 3145728 | tf_op jit(solution)/shard_map/reduce_scatter | solution.py:384
  467.5 181.9 %reduce-scatter.23.cloned.1.call-start = ((), (), s32[]{:S(2)}) async-start(), calls=%async_computation.24 | async-start | bytes 3145728 | tf_op jit(solution)/shard_map/reduce_scatter | solution.py:399
  502.3 147.2 %reduce-scatter.11.cloned.1.call-start = ((), (), s32[]{:S(2)}) async-start(), calls=%async_computation.18 | async-start | bytes 1572864 | tf_op jit(solution)/shard_map/reduce_scatter | solution.py:375
  626.0 42.2 %reduce-scatter.13.cloned.1.call-start = ((), (), s32[]{:S(2)}) async-start(), calls=%async_computation.19 | async-start | bytes 1572864 | tf_op jit(solution)/shard_map/reduce_scatter | solution.py:378
  627.6 114.8 %reduce-scatter.25.cloned.1.call-start = ((), (), s32[]{:S(2)}) async-start(), calls=%async_computation.25 | async-start | bytes 8650752 | tf_op jit(solution)/shard_map/reduce_scatter | solution.py:405
  631.9 184.7 %reduce-scatter.27.cloned.1.call-start = ((), (), s32[]{:S(2)}) async-start(), calls=%async_computation.26 | async-start | bytes 8650752 | tf_op jit(solution)/shard_map/reduce_scatter | solution.py:408
  637.2 253.6 %reduce-scatter.29.cloned.1.call-start = ((), (), s32[]{:S(2)}) async-start(), calls=%async_computation.27 | async-start | bytes 8650752 | tf_op jit(solution)/shard_map/reduce_scatter | solution.py:411
  642.6 282.8 %reduce-scatter.15.cloned.1.call-start = ((), (), s32[]{:S(2)}) async-start(), calls=%async_computation.20 | async-start | bytes 3145728 | tf_op jit(solution)/shard_map/reduce_scatter | solution.py:381
  646.6 296.4 %reduce-scatter.21.cloned.1.call-start = ((), (), s32[]{:S(2)}) async-start(), calls=%async_computation.23 | async-start | bytes 24576 | tf_op jit(solution)/shard_map/reduce_scatter | solution.py:390
  648.4 301.8 %reduce-scatter.19.cloned.1.call-start = ((), (), s32[]{:S(2)}) async-start(), calls=%async_computation.22 | async-start | bytes 49152 | tf_op jit(solution)/shard_map/reduce_scatter | solution.py:387
  649.4 545.5 %all-reduce.13.cloned.1.call-start = ((), (), s32[]{:S(2)}) async-start(), calls=%async_computation.30 | async-start | bytes 25690112 | tf_op jit(solution)/shard_map/psum | solution.py:417
  (118 other events, 1068.6 us)
Sparse Core Ops, SparseCore 0:
  9.6 24.1 all-gather.16
  35.4 21.2 all-gather.20
  58.2 33.0 all-gather.18
  92.8 33.0 all-gather.22
  128.5 50.5 all-gather.32
  180.5 31.6 all-gather.24
  213.7 74.4 all-gather.26
  289.7 74.4 all-gather.28
  365.8 74.4 all-gather.30
  459.4 50.3 all-gather.34
  512.6 30.4 reduce-scatter.16
  545.7 31.9 reduce-scatter.22
  626.1 18.9 reduce-scatter.10
  647.7 20.3 reduce-scatter.12
  670.9 71.4 reduce-scatter.24
  745.1 71.4 reduce-scatter.26
  819.3 71.4 reduce-scatter.28
  893.5 31.8 reduce-scatter.14
  928.2 9.9 reduce-scatter.20
  940.2 10.0 reduce-scatter.18
  955.7 239.0 all-reduce.12
where the time goes:
time: 1230 us; the launch traced here: 1220 us
  waiting for transfers between devices  765 us (62%)
  blocking collectives  146 us (12%)
  other arithmetic  87.8 us (7%)
  matrix products  86.1 us (7%)
  local copies, waits for them, and re-layouts  67.1 us (5%)
  loops' own time  48.7 us (4%)
  between operations  19 us (2%)
    psum x1, waiting for transfers between devices, per_device(): lax.psum(owned[1].astype(jnp.bfloat16), 'seq').astype(jnp.float32)  178 us
    reduce_scatter x1, waiting for transfers between devices, per_device(): lax.psum_scatter(grad_up.astype(jnp.bfloat16), 'batch', scatter_dimension...  74.2 us
    reduce_scatter x1, waiting for transfers between devices, per_device(): lax.psum_scatter(grad_gate.astype(jnp.bfloat16), 'batch', scatter_dimensi...  74.2 us
    reduce_scatter x1, waiting for transfers between devices, per_device(): lax.psum_scatter(grad_down.astype(jnp.bfloat16), 'batch', scatter_dimensi...  74.2 us
    all_gather x1, waiting for transfers between devices, per_device(): lax.all_gather(w_gate, 'batch', axis=0, tiled=True)  73.8 us
    all_gather x1, waiting for transfers between devices, per_device(): lax.all_gather(w_down, 'batch', axis=0, tiled=True)  71.4 us
    all_gather x1, waiting for transfers between devices, per_device(): lax.all_gather(w_up, 'batch', axis=0, tiled=True)  71.3 us
    psum x1, blocking collectives, per_device(): lax.psum(owned[0].astype(jnp.bfloat16), 'seq').astype(jnp.float32)  63.5 us
  transfers between devices with their start and end apart: 21, of which 15 were waited for; matrix products, arithmetic and copies ran while one was open for 16% of the time, Pallas kernels for 0%

commit v1 on v0

v1 whole, which is shorter than its diff:
```python
import jax
import jax.numpy as jnp
from jax import lax
from jax.sharding import PartitionSpec as P

HEADS = 4
DK = 128
DV = 256
SPAN = 64
KEYS = 512
VALS = 1024


norm_eps = 1e-05
head_eps = 0.1
top_prec = lax.Precision.HIGHEST
BOTH = ("batch", "seq")


def rms_scale(values_in):
    return lax.rsqrt(jnp.mean(values_in * values_in, axis=-1, keepdims=True) + norm_eps)


def head_rms(values_in):
    return lax.rsqrt(jnp.mean(values_in * values_in, axis=-1, keepdims=True) + head_eps)


def silu_grad(pre_act, sig_val):
    return sig_val * (1.0 + pre_act * (1.0 - sig_val))


def mm(eq, a, b):
    return jnp.einsum(eq, a, b, precision=top_prec)


def own_piece(shard):
    rows = shard.shape[0] // lax.axis_size("seq")
    return lax.dynamic_slice_in_dim(shard, lax.axis_index("seq") * rows, rows, 0)


def gather_rows(shards):
    pieces = [own_piece(shard) for shard in shards]
    piece = pieces[0] if len(pieces) == 1 else jnp.concatenate(pieces, axis=1)
    return lax.all_gather(piece, BOTH, axis=0, tiled=True)


def sum_rows(partial):
    piece = lax.psum_scatter(
        partial.astype(jnp.bfloat16), BOTH, scatter_dimension=0, tiled=True
    )
    return lax.all_gather(piece, "seq", axis=0, tiled=True)


def to_spans(array_in, width):
    return array_in.reshape(-1, SPAN, HEADS, width).transpose(0, 2, 1, 3)


def from_spans(array_in):
    spans, heads, span_len, width = array_in.shape
    return array_in.transpose(0, 2, 1, 3).reshape(spans * span_len, heads * width)


def per_device(
    inputs,
    seg_ids,
    gain_attn,
    w_query,
    w_key,
    w_value,
    w_outgate,
    w_rank_in,
    w_rank_out,
    rank_bias,
    head_gain,
    w_output,
    gain_ffn,
    w_gate,
    w_up,
    w_down,
    cotangent,
):
    f32 = jnp.float32
    bf16 = jnp.bfloat16
    nb = lax.axis_size("batch")
    mine_b = lax.axis_index("batch")
    place = lax.axis_index("seq")
    peers = lax.axis_size("seq")

    small = (gain_attn, gain_ffn, rank_bias, head_gain, w_rank_in, w_rank_out)
    packed = jnp.concatenate([a.reshape(-1) for a in small])
    packed = lax.all_gather(packed, "batch", axis=0)
    parts, at = [], 0
    for a in small:
        parts.append(packed[:, at : at + a.size])
        at += a.size
    gain_one = parts[0].reshape(-1).astype(f32)
    gain_two = parts[1].reshape(-1).astype(f32)
    bias_w = parts[2].reshape(-1).astype(f32)
    head_gain32 = parts[3].reshape(-1).astype(f32)
    rank_in_w = parts[4].reshape(-1, w_rank_in.shape[1])
    rank_out_w = (
        parts[5].reshape((nb,) + w_rank_out.shape).transpose(1, 0, 2)
        .reshape(w_rank_out.shape[0], -1)
        .astype(f32)
    )
    proj_w = gather_rows((w_query, w_key, w_value, w_outgate))
    output_w = gather_rows((w_output,)).reshape((nb,) + w_output.shape)
    gate_up_w = gather_rows((w_gate, w_up))
    down_w = gather_rows((w_down,))
    ff = w_gate.shape[1]

    activation = inputs[0].astype(f32)
    seg_row = seg_ids[0]
    tok_count = activation.shape[0]
    spans = tok_count // SPAN
    scale_one = rms_scale(activation)
    unit_one = activation * scale_one
    normed = (unit_one * gain_one).astype(bf16)

    low_rank = jnp.dot(normed, rank_in_w, preferred_element_type=f32)
    logits = jnp.dot(low_rank, rank_out_w, precision=top_prec) + bias_w
    decays = jax.nn.log_sigmoid(logits) / 16.0

    seg_s = seg_row.reshape(spans, SPAN)
    first_s, last_s = seg_s[:, 0], seg_s[:, -1]
    row_pos = lax.broadcasted_iota(jnp.int32, (SPAN, SPAN), 0)
    col_pos = lax.broadcasted_iota(jnp.int32, (SPAN, SPAN), 1)
    lower = (col_pos <= row_pos).astype(f32)
    allowed = lower[None] * (seg_s[:, :, None] == seg_s[:, None, :]).astype(f32)
    allowed = allowed[:, None]
    prior = jnp.concatenate([seg_row[:1], last_s[:-1]])
    enters = (first_s == prior).astype(f32)
    within = ((seg_s == first_s[:, None]).astype(f32) * enters[:, None])[:, None, :, None]
    end_doc = (seg_s == last_s[:, None]).astype(f32)[:, None, :, None]

    cumul = mm("ts,nsc->ntc", lower, decays.reshape(spans, SPAN, KEYS))
    total_log = jnp.sum(cumul[:, -1], axis=0)
    edges = jnp.stack([seg_row[0], seg_row[-1]]).astype(f32)
    notes = lax.all_gather(jnp.concatenate([total_log, edges]), "seq", axis=0)
    all_log, firsts, lasts = notes[:, :KEYS], notes[:, KEYS], notes[:, KEYS + 1]

    proj = jnp.dot(normed, proj_w, preferred_element_type=f32)
    queries = to_spans(proj[:, :KEYS] * DK ** (-0.5), DK)
    keys_s = to_spans(proj[:, KEYS : 2 * KEYS], DK)
    values_s = to_spans(proj[:, 2 * KEYS : 2 * KEYS + VALS], DV)
    outgate = proj[:, 2 * KEYS + VALS :]

    cumul = cumul.reshape(spans, SPAN, HEADS, DK).transpose(0, 2, 1, 3)
    last_cumul = cumul[:, :, -1:, :]
    grow = jnp.exp(cumul)
    shrink = jnp.exp(-cumul)
    to_end = jnp.exp(last_cumul - cumul) * end_doc
    query_dec = queries * grow
    key_dec = keys_s * shrink
    key_end = keys_s * to_end
    query_in = query_dec * within
    keep = jnp.exp(last_cumul[:, :, 0, :]) * within[:, :, -1]
    scores = mm("nhtc,nhsc->nhts", query_dec, key_dec) * allowed
    local_out = mm("nhts,nhsv->nhtv", scores, values_s)
    added = mm("nhsc,nhsv->nhcv", key_end, values_s)

    local_state = added[0]
    for i in range(1, spans):
        local_state = keep[i][:, :, None] * local_state + added[i]
    states = lax.all_gather(local_state.astype(bf16), "seq", axis=0)

    before = lax.broadcasted_iota(jnp.int32, (peers, peers), 1)
    row = lax.broadcasted_iota(jnp.int32, (peers, peers), 0)
    order = jnp.arange(peers)
    between = jnp.logical_and(before > row, before < place).astype(f32)
    reach = jnp.logical_and(order < place, lasts == edges[0]).astype(f32)
    weight = jnp.exp(mm("ji,ic->jc", between, all_log)) * reach[:, None]
    carried = jnp.sum(
        states.astype(f32) * weight.reshape(peers, HEADS, DK, 1), axis=0
    )
    enter_list = [carried]
    for i in range(spans - 1):
        enter_list.append(keep[i][:, :, None] * enter_list[i] + added[i])
    entered = jnp.stack(enter_list)

    attn_raw = from_spans(local_out + mm("nhtc,nhcv->nhtv", query_in, entered)).reshape(
        tok_count, HEADS, DV
    )
    head_scale = head_rms(attn_raw)
    head_norm = attn_raw * head_scale
    gate_h = outgate.reshape(tok_count, HEADS, DV)
    gate_sig = jax.nn.sigmoid(gate_h)
    gate_act = gate_h * gate_sig
    gated = (head_norm * head_gain32 * gate_act).reshape(tok_count, VALS).astype(bf16)
    out_proj = jnp.concatenate(
        [jnp.dot(gated, output_w[b], preferred_element_type=f32) for b in range(nb)], axis=1
    )
    resid = activation + out_proj
    scale_two = rms_scale(resid)
    unit_two = resid * scale_two
    normed_two = (unit_two * gain_two).astype(bf16)
    gate_up = jnp.dot(normed_two, gate_up_w, preferred_element_type=f32)
    gate_pre, up_pre = gate_up[:, :ff], gate_up[:, ff:]
    ffn_sig = jax.nn.sigmoid(gate_pre)
    hidden = (gate_pre * ffn_sig * up_pre).astype(bf16)
    output = (resid + jnp.dot(hidden, down_w, preferred_element_type=f32)).astype(bf16)

    cot_rows = cotangent[0]
    grad_down = sum_rows(jnp.dot(hidden.T, cot_rows, preferred_element_type=f32))
    grad_hidden = jnp.dot(cot_rows, down_w.T, preferred_element_type=f32)
    grad_gate_up = jnp.concatenate(
        [
            (grad_hidden * up_pre * silu_grad(gate_pre, ffn_sig)).astype(bf16),
            (grad_hidden * gate_pre * ffn_sig).astype(bf16),
        ],
        axis=1,
    )
    grad_gu = sum_rows(jnp.dot(normed_two.T, grad_gate_up, preferred_element_type=f32))
    grad_normed_two = jnp.dot(grad_gate_up, gate_up_w.T, preferred_element_type=f32)
    grad_gain_two = jnp.sum(grad_normed_two * unit_two, axis=0)
    scaled_two = grad_normed_two * gain_two
    grad_resid = cot_rows.astype(f32) + scale_two * (
        scaled_two - unit_two * jnp.mean(scaled_two * unit_two, axis=-1, keepdims=True)
    )
    resid_bf = grad_resid.astype(bf16)
    half = resid_bf.shape[1] // nb
    halves = [resid_bf[:, b * half : (b + 1) * half] for b in range(nb)]
    grad_output = sum_rows(
        jnp.concatenate(
            [jnp.dot(gated.T, part, preferred_element_type=f32) for part in halves], axis=0
        )
    )
    grad_gated = sum(
        jnp.dot(part, output_w[b].T, preferred_element_type=f32)
        for b, part in enumerate(halves)
    ).reshape(tok_count, HEADS, DV)
    grad_headgain = jnp.sum(grad_gated * head_norm * gate_act, axis=(0, 1))
    grad_gate_h = grad_gated * head_norm * head_gain32 * silu_grad(gate_h, gate_sig)
    grad_norm_h = grad_gated * head_gain32 * gate_act
    grad_attn = head_scale * (
        grad_norm_h - head_norm * jnp.mean(grad_norm_h * head_norm, axis=-1, keepdims=True)
    )
    grad_o = to_spans(grad_attn.reshape(tok_count, VALS), DV)

    reach_grad = mm("nhtc,nhtv->nhcv", query_in, grad_o)
    local_grad = reach_grad[spans - 1]
    for i in range(spans - 2, -1, -1):
        local_grad = keep[i][:, :, None] * local_grad + reach_grad[i]
    grads_in = lax.all_gather(local_grad.astype(bf16), "seq", axis=0)

    grad_scores = mm("nhtv,nhsv->nhts", grad_o, values_s) * allowed
    grad_qd = mm("nhts,nhsc->nhtc", grad_scores, key_dec)
    grad_qd = grad_qd + within * mm("nhtv,nhcv->nhtc", grad_o, entered)
    grad_kd = mm("nhts,nhtc->nhsc", grad_scores, query_dec)
    grad_v = mm("nhts,nhtv->nhsv", scores, grad_o)

    between = jnp.logical_and(before < row, before > place).astype(f32)
    reach = jnp.logical_and(order > place, firsts == edges[1]).astype(f32)
    weight = jnp.exp(mm("ji,ic->jc", between, all_log)) * reach[:, None]
    grad_end = jnp.sum(
        grads_in.astype(f32) * weight.reshape(peers, HEADS, DK, 1), axis=0
    )
    end_list = [grad_end]
    for i in range(spans - 1, 0, -1):
        end_list.append(keep[i][:, :, None] * end_list[-1] + reach_grad[i])
    ends = jnp.stack(end_list[::-1])

    grad_v = grad_v + mm("nhsc,nhcv->nhsv", key_end, ends)
    grad_ke = mm("nhsv,nhcv->nhsc", values_s, ends)
    moved = grad_ke * key_end
    grad_last = jnp.sum(moved, axis=2) + keep * jnp.sum(ends * entered, axis=3)
    grad_cumul = grad_qd * query_dec - grad_kd * key_dec - moved
    grad_d = mm("ts,nhtc->nhsc", lower, grad_cumul) + grad_last[:, :, None, :]
    grad_q = grad_qd * grow
    grad_k = grad_kd * shrink + grad_ke * to_end

    grad_logits = from_spans(grad_d) * jax.nn.sigmoid(-logits) / 16.0
    grad_bias = jnp.sum(grad_logits, axis=0)
    grad_rank_out = jnp.dot(low_rank.T, grad_logits, precision=top_prec)
    grad_low = jnp.dot(grad_logits, rank_out_w.T, precision=top_prec).astype(bf16)
    proj_grad = jnp.concatenate(
        [
            from_spans(grad_q * DK ** (-0.5)).astype(bf16),
            from_spans(grad_k).astype(bf16),
            from_spans(grad_v).astype(bf16),
            grad_gate_h.reshape(tok_count, VALS).astype(bf16),
        ],
        axis=1,
    )
    grad_proj = sum_rows(jnp.dot(normed.T, proj_grad, preferred_element_type=f32))
    grad_normed = jnp.dot(proj_grad, proj_w.T, preferred_element_type=f32) + jnp.dot(
        grad_low, rank_in_w.T, preferred_element_type=f32
    )
    grad_gain_one = jnp.sum(grad_normed * unit_one, axis=0)
    scaled_one = grad_normed * gain_one
    grad_input = (
        grad_resid
        + scale_one
        * (scaled_one - unit_one * jnp.mean(scaled_one * unit_one, axis=-1, keepdims=True))
    ).astype(bf16)
    grad_rank_in = jnp.dot(normed.T, grad_low, preferred_element_type=f32)

    by_owner = jnp.concatenate(
        [
            grad_gain_one.reshape(nb, -1),
            grad_gain_two.reshape(nb, -1),
            grad_bias.reshape(nb, -1),
            grad_headgain.reshape(nb, -1),
            grad_rank_in.reshape(nb, -1),
            grad_rank_out.reshape(w_rank_out.shape[0], nb, -1).transpose(1, 0, 2).reshape(nb, -1),
        ],
        axis=1,
    )
    owned = lax.dynamic_index_in_dim(lax.psum(by_owner, BOTH), mine_b, 0, False)
    outs, at = [], 0
    for a in small:
        outs.append(owned[at : at + a.size].reshape(a.shape))
        at += a.size
    g_gain_one, g_gain_two, g_bias, g_headgain, g_rank_in, g_rank_out = outs
    grad_proj = grad_proj.astype(f32)
    grad_gu = grad_gu.astype(f32)
    return (
        output[None],
        grad_input[None],
        g_gain_one,
        grad_proj[:, :KEYS],
        grad_proj[:, KEYS : 2 * KEYS],
        grad_proj[:, 2 * KEYS : 2 * KEYS + VALS],
        grad_proj[:, 2 * KEYS + VALS :],
        g_rank_in,
        g_rank_out,
        g_bias,
        g_headgain,
        grad_output.astype(f32),
        g_gain_two,
        grad_gu[:, :ff],
        grad_gu[:, ff:],
        grad_down.astype(f32),
    )


def solution(mesh):
    in_specs = (
        P("batch", "seq", None),
        P("batch", "seq"),
        P("batch"),
        P("batch", None),
        P("batch", None),
        P("batch", None),
        P("batch", None),
        P("batch", None),
        P(None, "batch"),
        P("batch"),
        P("batch"),
        P(None, "batch"),
        P("batch"),
        P("batch", None),
        P("batch", None),
        P("batch", None),
        P("batch", "seq", None),
    )
    out_specs = (
        P("batch", "seq", None),
        P("batch", "seq", None),
        P("batch"),
        P("batch", None),
        P("batch", None),
        P("batch", None),
        P("batch", None),
        P("batch", None),
        P(None, "batch"),
        P("batch"),
        P("batch"),
        P(None, "batch"),
        P("batch"),
        P("batch", None),
        P("batch", None),
        P("batch", None),
    )
    return jax.shard_map(
        per_device, mesh=mesh, in_specs=in_specs, out_specs=out_specs, check_vma=False
    )
```

time: 1230 us -> 1350 us (1.098)
  waiting for transfers between devices: 765 us -> 1080 us
  blocking collectives: 146 us -> 67.1 us
  loops' own time: 48.7 us -> 0 us
  other arithmetic: 87.8 us -> 40.7 us
    reduce_scatter x10 -> x4, waiting for transfers between devices: 283 us -> 525 us  [sum_rows(): lax.psum_scatter(partial.astype(jnp.bfloat16), BOTH, scatter_dimension=0,...]
    all_gather x10, waiting for transfers between devices: 299 us -> 428 us  [the longest x4 222 us: gather_rows(): return lax.all_gather(piece, BOTH, axis=0, tiled=True)]
    psum x1 -> x0, blocking collectives: 63.5 us -> none  [per_device(): lax.psum(owned[0].astype(jnp.bfloat16), 'seq').astype(jnp.float32)]
    psum x1, waiting for transfers between devices: 178 us -> 124 us  [per_device(): owned = lax.dynamic_index_in_dim(lax.psum(by_owner, BOTH), mine_b, 0, False)]
    another operation x5 -> x0, loops' own time: 48.7 us -> none  [the longest x1 42.5 us: entering(): return lax.fori_loop(0, peers, turn, start)]
    all_gather x7 -> x1, blocking collectives: 44.6 us -> 5.75 us  [per_device(): packed = lax.all_gather(packed, 'batch', axis=0)]
    unnamed x2 -> x1, blocking collectives: 38.3 us -> 61.4 us
    dynamic_slice x50 -> x5, local copies, waits for them, and re-layouts: 24.7 us -> 5.03 us  [own_piece(): lax.dynamic_slice_in_dim(shard, lax.axis_index('seq') * rows, rows, 0)]
  transfers between devices with their start and end apart: 21 -> 15, of which waited for: 15 -> 14; matrix products, arithmetic and copies ran while one was open for 16% -> 9% of each run, Pallas kernels for 0% -> 0%
where the time goes in v1:
time: 1350 us; the launch traced here: 1340 us
  waiting for transfers between devices  1080 us (80%)
  matrix products  79.4 us (6%)
  blocking collectives  67.1 us (5%)
  local copies, waits for them, and re-layouts  60.4 us (4%)
  other arithmetic  40.7 us (3%)
  between operations  16.3 us (1%)
    reduce_scatter x4, waiting for transfers between devices, sum_rows(): lax.psum_scatter(partial.astype(jnp.bfloat16), BOTH, scatter_dimension=0,...  525 us
    all_gather x4, waiting for transfers between devices, gather_rows(): return lax.all_gather(piece, BOTH, axis=0, tiled=True)  222 us
    all_gather x4, waiting for transfers between devices, sum_rows(): return lax.all_gather(piece, 'seq', axis=0, tiled=True)  170 us
    psum x1, waiting for transfers between devices, per_device(): owned = lax.dynamic_index_in_dim(lax.psum(by_owner, BOTH), mine_b, 0, False)  124 us
    unnamed x1, blocking collectives  61.4 us
    all_gather x1, waiting for transfers between devices, per_device(): grads_in = lax.all_gather(local_grad.astype(bf16), 'seq', axis=0)  35.5 us
  transfers between devices with their start and end apart: 15, of which 14 were waited for; matrix products, arithmetic and copies ran while one was open for 9% of the time, Pallas kernels for 0%

profile of v1, /device:TPU:0, one launch (start us, length us, event | category | flops | bytes accessed | tf_op | source)
XLA Modules:
  0.0 1341.2 jit_solution(14421822726846353848)
XLA Ops:
  15.6 5.7 all-gather.2
  32.2 51.4 %all-gather.14.cloned.1.call-done = bf16[1024,3072]{1,0:T(8,128)(2,1)} async-done(((bf16[32,3072]{1,0:T(8,128)(2,1)}), bf16[1024,3072]{1,0:T(8,128)(2,1)}) %all-gather.14.cloned.1.call-update) | async-done | bytes 6291472 | tf_op jit(solution)/shard_map/all_gather | solution.py:44
  108.8 61.4 %all-reduce = f32[8224]{0:T(1024)S(1)} all-reduce(f32[8224]{0:T(1024)S(1)} %maximum_dynamic-update-slice_fusion), channel_id=3, replica_groups=mesh['batch'=2,'seq'=16] {'seq'}, use_global_device_ids=true, to_apply=%add | all-reduce | flops 8224 | bytes 65792
  189.8 20.0 %all-gather.18.cloned.1.call-done = bf16[2048,512]{1,0:T(8,128)(2,1)} async-done(((bf16[64,512]{1,0:T(8,128)(2,1)}), bf16[2048,512]{1,0:T(8,128)(2,1)}) %all-gather.18.cloned.1.call-update) | async-done | bytes 2097168 | tf_op jit(solution)/shard_map/all_gather | solution.py:44
  213.2 89.3 %all-gather.20.cloned.1.call-done = bf16[1024,5632]{1,0:T(8,128)(2,1)} async-done(((bf16[32,5632]{1,0:T(8,128)(2,1)}), bf16[1024,5632]{1,0:T(8,128)(2,1)}) %all-gather.20.cloned.1.call-update) | async-done | bytes 11534352 | tf_op jit(solution)/shard_map/all_gather | solution.py:44
  302.4 7.6 fusion.124
  310.0 61.6 %all-gather.22.cloned.1.call-done = bf16[2816,1024]{1,0:T(8,128)(2,1)} async-done(((bf16[88,1024]{1,0:T(8,128)(2,1)}), bf16[2816,1024]{1,0:T(8,128)(2,1)}) %all-gather.22.cloned.1.call-update) | async-done | bytes 5767184 | tf_op jit(solution)/shard_map/all_gather | solution.py:44
  371.7 6.8 multiply_convert_fusion.1
  403.1 5.3 convolution_convert_fusion.1
  414.1 35.5 %all-gather.24.cloned.1.call-done = bf16[16,4,128,256]{3,2,1,0:T(8,128)(2,1)} async-done(((bf16[1,4,128,256]{3,2,1,0:T(8,128)(2,1)}), bf16[16,4,128,256]{3,2,1,0:T(8,128)(2,1)}) %all-gather.24.cloned.1.call-update) | async-done | bytes 4194320 | tf_op jit(solution)/shard_map/all_gather | solution.py:244
  457.5 4.5 convolution_convert_fusion.2
  463.1 7.1 convolution_convert_fusion
  471.0 118.4 %reduce-scatter.7.cloned.1.call-done = bf16[64,512]{1,0:T(8,128)(2,1)} async-done(((bf16[2048,512]{1,0:T(8,128)(2,1)}), bf16[64,512]{1,0:T(8,128)(2,1)}) %reduce-scatter.7.cloned.1.call-update) | async-done | bytes 65552 | tf_op jit(solution)/shard_map/reduce_scatter | solution.py:48
  593.4 5.1 fusion.90
  600.4 133.5 %reduce-scatter.11.cloned.1.call-done = bf16[88,1024]{1,0:T(8,128)(2,1)} async-done(((bf16[2816,1024]{1,0:T(8,128)(2,1)}), bf16[88,1024]{1,0:T(8,128)(2,1)}) %reduce-scatter.11.cloned.1.call-update) | async-done | bytes 180240 | tf_op jit(solution)/shard_map/reduce_scatter | solution.py:48
  734.0 116.5 %reduce-scatter.5.cloned.1.call-done = bf16[32,3072]{1,0:T(8,128)(2,1)} async-done(((bf16[1024,3072]{1,0:T(8,128)(2,1)}), bf16[32,3072]{1,0:T(8,128)(2,1)}) %reduce-scatter.5.cloned.1.call-update) | async-done | bytes 196624 | tf_op jit(solution)/shard_map/reduce_scatter | solution.py:48
  850.5 156.2 %reduce-scatter.9.cloned.1.call-done = bf16[32,5632]{1,0:T(8,128)(2,1)} async-done(((bf16[1024,5632]{1,0:T(8,128)(2,1)}), bf16[32,5632]{1,0:T(8,128)(2,1)}) %reduce-scatter.9.cloned.1.call-update) | async-done | bytes 360464 | tf_op jit(solution)/shard_map/reduce_scatter | solution.py:48
  1011.1 34.9 %all-gather.28.cloned.1.call-done = bf16[1024,512]{1,0:T(8,128)(2,1)} async-done(((bf16[64,512]{1,0:T(8,128)(2,1)}), bf16[1024,512]{1,0:T(8,128)(2,1)}) %all-gather.28.cloned.1.call-update) | async-done | bytes 1048592 | tf_op jit(solution)/shard_map/all_gather | solution.py:51
  1049.8 123.7 %all-reduce.3.cloned.1.call-done = f32[2,13696]{1,0:T(2,128)} async-done(((f32[2,13696]{1,0:T(2,128)}), f32[2,13696]{1,0:T(2,128)}) %all-reduce.3.cloned.1.call-update) | async-done | bytes 109584 | tf_op jit(solution)/shard_map/psum | solution.py:309
  1180.8 39.9 %all-gather.32.cloned.1.call-done = bf16[1408,1024]{1,0:T(8,128)(2,1)} async-done(((bf16[88,1024]{1,0:T(8,128)(2,1)}), bf16[1408,1024]{1,0:T(8,128)(2,1)}) %all-gather.32.cloned.1.call-update) | async-done | bytes 2883600 | tf_op jit(solution)/shard_map/all_gather | solution.py:51
  1220.7 5.1 convert_element_type.220
  1225.8 41.2 %all-gather.26.cloned.1.call-done = bf16[512,3072]{1,0:T(8,128)(2,1)} async-done(((bf16[32,3072]{1,0:T(8,128)(2,1)}), bf16[512,3072]{1,0:T(8,128)(2,1)}) %all-gather.26.cloned.1.call-update) | async-done | bytes 3145744 | tf_op jit(solution)/shard_map/all_gather | solution.py:51
  1272.4 53.7 %all-gather.30.cloned.1.call-done = bf16[512,5632]{1,0:T(8,128)(2,1)} async-done(((bf16[32,5632]{1,0:T(8,128)(2,1)}), bf16[512,5632]{1,0:T(8,128)(2,1)}) %all-gather.30.cloned.1.call-update) | async-done | bytes 5767184 | tf_op jit(solution)/shard_map/all_gather | solution.py:51
  1326.1 8.1 fusion.135
  (360 shorter events, 132.2 us)
Async XLA Ops:
  7.2 97.9 %copy-start = (bf16[1408,1024]{1,0:T(8,128)(2,1)S(1)}, bf16[1408,1024]{1,0:T(8,128)(2,1)}, u32[]{:S(2)}) copy-start(bf16[1408,1024]{1,0:T(8,128)(2,1)} %param.32) | copy-start | bytes 8650756
  7.2 76.4 %copy-start.3 = (bf16[1,128,1024]{2,1,0:T(8,128)(2,1)S(1)}, bf16[1,128,1024]{2,1,0:T(8,128)(2,1)}, u32[]{:S(2)}) copy-start(bf16[1,128,1024]{2,1,0:T(8,128)(2,1)} %param.17) | copy-start | bytes 786436
  7.2 76.3 %all-gather.14.cloned.1.call-start = ((), (), s32[]{:S(2)}) async-start(), calls=%async_computation.4 | async-start | bytes 6488064 | tf_op jit(solution)/shard_map/all_gather | solution.py:44
  9.8 168.8 %all-gather.16.cloned.1.call-start = ((), (), s32[]{:S(2)}) async-start(), calls=%async_computation.5 | async-start | bytes 4456448 | tf_op jit(solution)/shard_map/all_gather | solution.py:165
  101.6 108.1 %all-gather.18.cloned.1.call-start = ((), (), s32[]{:S(2)}) async-start(), calls=%async_computation.6 | async-start | bytes 2162688 | tf_op jit(solution)/shard_map/all_gather | solution.py:44
  103.2 199.3 %all-gather.20.cloned.1.call-start = ((), (), s32[]{:S(2)}) async-start(), calls=%async_computation.7 | async-start | bytes 11894784 | tf_op jit(solution)/shard_map/all_gather | solution.py:44
  105.0 266.6 %all-gather.22.cloned.1.call-start = ((), (), s32[]{:S(2)}) async-start(), calls=%async_computation.8 | async-start | bytes 5947392 | tf_op jit(solution)/shard_map/all_gather | solution.py:44
  105.8 343.8 %all-gather.24.cloned.1.call-start = ((), (), s32[]{:S(2)}) async-start(), calls=%async_computation.9 | async-start | bytes 4456448 | tf_op jit(solution)/shard_map/all_gather | solution.py:244
  173.7 223.7 %copy-start.69 = (f32[2,64]{1,0:T(2,128)}, f32[2,64]{1,0:T(2,128)S(1)}, u32[]{:S(2)}) copy-start(f32[2,64]{1,0:T(2,128)S(1)} %compare_select_fusion.3) | copy-start | bytes 1540
  213.1 169.8 %copy-start.64 = (f32[128]{0:T(128)}, f32[128]{0:T(128)S(1)}, u32[]{:S(2)}) copy-start(f32[128]{0:T(128)S(1)} %add_rsqrt_fusion.1) | copy-start | bytes 1540
  400.4 188.9 %reduce-scatter.7.cloned.1.call-start = ((), (), s32[]{:S(2)}) async-start(), calls=%async_computation.13 | async-start | bytes 2162688 | tf_op jit(solution)/shard_map/reduce_scatter | solution.py:48
  402.9 331.0 %reduce-scatter.11.cloned.1.call-start = ((), (), s32[]{:S(2)}) async-start(), calls=%async_computation.17 | async-start | bytes 5947392 | tf_op jit(solution)/shard_map/reduce_scatter | solution.py:48
  408.5 442.0 %reduce-scatter.5.cloned.1.call-start = ((), (), s32[]{:S(2)}) async-start(), calls=%async_computation.11 | async-start | bytes 6488064 | tf_op jit(solution)/shard_map/reduce_scatter | solution.py:48
  462.0 544.7 %reduce-scatter.9.cloned.1.call-start = ((), (), s32[]{:S(2)}) async-start(), calls=%async_computation.15 | async-start | bytes 11894784 | tf_op jit(solution)/shard_map/reduce_scatter | solution.py:48
  470.2 119.4 %copy-start.13 = (f32[1,4,128,256]{3,2,1,0:T(8,128)S(1)}, f32[1,4,128,256]{3,2,1,0:T(8,128)}, u32[]{:S(2)}) copy-start(f32[1,4,128,256]{3,2,1,0:T(8,128)} %copy-done.11) | copy-start | bytes 1572868
  470.2 119.4 %copy-start.15 = (f32[1,4,128,256]{3,2,1,0:T(8,128)S(1)}, f32[1,4,128,256]{3,2,1,0:T(8,128)}, u32[]{:S(2)}) copy-start(f32[1,4,128,256]{3,2,1,0:T(8,128)} %copy-done.14) | copy-start | bytes 1572868
  470.3 119.7 %copy-start.77 = (f32[2]{0:T(128)S(1)}, f32[2]{0:T(128)}, u32[]{:S(2)}) copy-start(f32[2]{0:T(128)} %copy-done.76) | copy-start | bytes 28
  470.3 122.5 %copy-start.59 = (bf16[2,8,2,256]{3,1,2,0:T(8,128)(2,1)S(1)}, bf16[2,8,2,256]{3,1,2,0:T(8,128)(2,1)}, u32[]{:S(2)}) copy-start(bf16[2,8,2,256]{3,1,2,0:T(8,128)(2,1)} %copy-done.58) | copy-start | bytes 49156
  470.3 575.6 %all-gather.28.cloned.1.call-start = ((), (), s32[]{:S(2)}) async-start(), calls=%async_computation.14 | async-start | bytes 1114112 | tf_op jit(solution)/shard_map/all_gather | solution.py:51
  589.4 584.2 %all-reduce.3.cloned.1.call-start = ((), (), s32[]{:S(2)}) async-start(), calls=%async_computation.10 | async-start | bytes 219136 | tf_op jit(solution)/shard_map/psum | solution.py:309
  598.6 408.2 %copy-start.23 = (bf16[128,2816]{1,0:T(8,128)(2,1)S(1)}, bf16[128,2816]{1,0:T(8,128)(2,1)}, u32[]{:S(2)}) copy-start(bf16[128,2816]{1,0:T(8,128)(2,1)} %get-tuple-element.102) | copy-start | bytes 2162692
  600.3 620.4 %all-gather.32.cloned.1.call-start = ((), (), s32[]{:S(2)}) async-start(), calls=%async_computation.18 | async-start | bytes 3063808 | tf_op jit(solution)/shard_map/all_gather | solution.py:51
  733.9 533.0 %all-gather.26.cloned.1.call-start = ((), (), s32[]{:S(2)}) async-start(), calls=%async_computation.12 | async-start | bytes 3342336 | tf_op jit(solution)/shard_map/all_gather | solution.py:51
  850.5 475.6 %all-gather.30.cloned.1.call-start = ((), (), s32[]{:S(2)}) async-start(), calls=%async_computation.16 | async-start | bytes 6127616 | tf_op jit(solution)/shard_map/all_gather | solution.py:51
  (73 other events, 704.0 us)
Sparse Core Ops, SparseCore 0:
  11.5 72.0 all-gather.13
  101.7 49.5 all-gather.15
  154.8 54.8 all-gather.17
  213.0 89.3 all-gather.19
  305.7 65.8 all-gather.21
  400.5 49.0 all-gather.23
  452.4 136.8 reduce-scatter.6
  592.2 141.6 reduce-scatter.10
  739.5 110.8 reduce-scatter.4
  852.6 154.0 reduce-scatter.8
  1008.9 36.9 all-gather.27
  1051.9 121.5 all-reduce.2
  1175.8 44.8 all-gather.31
  1222.9 44.0 all-gather.25
  1269.1 56.9 all-gather.29

commit v2 on v1

--- a/solution.py
+++ b/solution.py
@@ -33,22 +33,23 @@
     return jnp.einsum(eq, a, b, precision=top_prec)
 
 
-def own_piece(shard):
-    rows = shard.shape[0] // lax.axis_size("seq")
-    return lax.dynamic_slice_in_dim(shard, lax.axis_index("seq") * rows, rows, 0)
-
-
 def gather_rows(shards):
-    pieces = [own_piece(shard) for shard in shards]
-    piece = pieces[0] if len(pieces) == 1 else jnp.concatenate(pieces, axis=1)
-    return lax.all_gather(piece, BOTH, axis=0, tiled=True)
-
-
-def sum_rows(partial):
-    piece = lax.psum_scatter(
-        partial.astype(jnp.bfloat16), BOTH, scatter_dimension=0, tiled=True
-    )
-    return lax.all_gather(piece, "seq", axis=0, tiled=True)
+    piece = shards[0] if len(shards) == 1 else jnp.concatenate(shards, axis=1)
+    return lax.all_gather(piece, "batch", axis=0, tiled=True)
+
+
+def all_tokens(rows):
+    return lax.all_gather(rows, "batch", axis=0, tiled=True)
+
+
+def own_columns(rows):
+    width = rows.shape[1] // lax.axis_size("batch")
+    return lax.dynamic_slice_in_dim(rows, lax.axis_index("batch") * width, width, 1)
+
+
+def own_grad(left, right):
+    part = jnp.dot(left.T, right, preferred_element_type=jnp.float32)
+    return lax.psum(part.astype(jnp.bfloat16), "seq")
 
 
 def to_spans(array_in, width):
@@ -201,7 +202,7 @@
     output = (resid + jnp.dot(hidden, down_w, preferred_element_type=f32)).astype(bf16)
 
     cot_rows = cotangent[0]
-    grad_down = sum_rows(jnp.dot(hidden.T, cot_rows, preferred_element_type=f32))
+    grad_down = own_grad(own_columns(all_tokens(hidden)), all_tokens(cot_rows))
     grad_hidden = jnp.dot(cot_rows, down_w.T, preferred_element_type=f32)
     grad_gate_up = jnp.concatenate(
         [
@@ -210,7 +211,7 @@
         ],
         axis=1,
     )
-    grad_gu = sum_rows(jnp.dot(normed_two.T, grad_gate_up, preferred_element_type=f32))
+    grad_gu = own_grad(own_columns(all_tokens(normed_two)), all_tokens(grad_gate_up))
     grad_normed_two = jnp.dot(grad_gate_up, gate_up_w.T, preferred_element_type=f32)
     grad_gain_two = jnp.sum(grad_normed_two * unit_two, axis=0)
     scaled_two = grad_normed_two * gain_two
@@ -220,11 +221,7 @@
     resid_bf = grad_resid.astype(bf16)
     half = resid_bf.shape[1] // nb
     halves = [resid_bf[:, b * half : (b + 1) * half] for b in range(nb)]
-    grad_output = sum_rows(
-        jnp.concatenate(
-            [jnp.dot(gated.T, part, preferred_element_type=f32) for part in halves], axis=0
-        )
-    )
+    grad_output = own_grad(all_tokens(gated), own_columns(all_tokens(resid_bf)))
     grad_gated = sum(
         jnp.dot(part, output_w[b].T, preferred_element_type=f32)
         for b, part in enumerate(halves)
@@ -282,7 +279,7 @@
         ],
         axis=1,
     )
-    grad_proj = sum_rows(jnp.dot(normed.T, proj_grad, preferred_element_type=f32))
+    grad_proj = own_grad(own_columns(all_tokens(normed)), all_tokens(proj_grad))
     grad_normed = jnp.dot(proj_grad, proj_w.T, preferred_element_type=f32) + jnp.dot(
         grad_low, rank_in_w.T, preferred_element_type=f32
     )

time: 1350 us -> 999 us (0.74)
  waiting for transfers between devices: 1080 us -> 686 us
  blocking collectives: 67.1 us -> 134 us
  local copies, waits for them, and re-layouts: 60.4 us -> 38.5 us
    reduce_scatter x4 -> x0, waiting for transfers between devices: 525 us -> none  [sum_rows(): lax.psum_scatter(partial.astype(jnp.bfloat16), BOTH, scatter_dimension=0,...]
    psum x0 -> x1, waiting for transfers between devices: none -> 237 us  [own_grad(): return lax.psum(part.astype(jnp.bfloat16), 'seq')]
    all_gather x8 -> x7, waiting for transfers between devices: 392 us -> 294 us  [the longest x4 270 us: gather_rows(): return lax.all_gather(piece, 'batch', axis=0, tiled=True)]
    all_gather x0 -> x5, blocking collectives: none -> 65.4 us  [all_tokens(): return lax.all_gather(rows, 'batch', axis=0, tiled=True)]
  transfers between devices with their start and end apart: 15 -> 11, of which waited for: 14 -> 7; matrix products, arithmetic and copies ran while one was open for 9% -> 10% of each run, Pallas kernels for 0% -> 0%
where the time goes in v2:
time: 999 us; the launch traced here: 993 us
  waiting for transfers between devices  686 us (69%)
  blocking collectives  134 us (13%)
  matrix products  73.4 us (7%)
  other arithmetic  43.9 us (4%)
  local copies, waits for them, and re-layouts  38.5 us (4%)
  between operations  16.2 us (2%)
    all_gather x4, waiting for transfers between devices, gather_rows(): return lax.all_gather(piece, 'batch', axis=0, tiled=True)  270 us
    psum x1, waiting for transfers between devices, own_grad(): return lax.psum(part.astype(jnp.bfloat16), 'seq')  237 us
    psum x1, waiting for transfers between devices, per_device(): owned = lax.dynamic_index_in_dim(lax.psum(by_owner, BOTH), mine_b, 0, False)  118 us
    all_gather x5, blocking collectives, all_tokens(): return lax.all_gather(rows, 'batch', axis=0, tiled=True)  65.4 us
    unnamed x1, blocking collectives  62.5 us
    all_gather x1, waiting for transfers between devices, per_device(): grads_in = lax.all_gather(local_grad.astype(bf16), 'seq', axis=0)  35.4 us
    all_gather x3, waiting for transfers between devices, all_tokens(): return lax.all_gather(rows, 'batch', axis=0, tiled=True)  24.4 us
  transfers between devices with their start and end apart: 11, of which 7 were waited for; matrix products, arithmetic and copies ran while one was open for 10% of the time, Pallas kernels for 0%

profile of v2, /device:TPU:0, one launch (start us, length us, event | category | flops | bytes accessed | tf_op | source)
XLA Modules:
  0.0 992.6 jit_solution(13083778052164014564)
XLA Ops:
  13.0 5.7 all-gather.3
  27.2 66.5 %all-gather.14.cloned.1.call-done = bf16[1024,3072]{1,0:T(8,128)(2,1)} async-done(((bf16[512,3072]{1,0:T(8,128)(2,1)}), bf16[1024,3072]{1,0:T(8,128)(2,1)}) %all-gather.14.cloned.1.call-update) | async-done | bytes 6291472 | tf_op jit(solution)/shard_map/all_gather | solution.py:38
  102.0 5.6 pad_maximum_fusion
  112.4 62.5 %all-reduce = f32[8224]{0:T(1024)S(1)} all-reduce(f32[8224]{0:T(1024)S(1)} %maximum_dynamic-update-slice_fusion), channel_id=3, replica_groups=mesh['batch'=2,'seq'=16] {'seq'}, use_global_device_ids=true, to_apply=%add | all-reduce | flops 8224 | bytes 65792
  193.8 134.9 %all-gather.20.cloned.1.call-done = bf16[1024,5632]{1,0:T(8,128)(2,1)} async-done(((bf16[512,5632]{1,0:T(8,128)(2,1)}), bf16[1024,5632]{1,0:T(8,128)(2,1)}) %all-gather.20.cloned.1.call-update) | async-done | bytes 11534352 | tf_op jit(solution)/shard_map/all_gather | solution.py:38
  328.7 7.5 fusion.140
  336.2 68.3 %all-gather.22.cloned.1.call-done = bf16[2816,1024]{1,0:T(8,128)(2,1)} async-done(((bf16[1408,1024]{1,0:T(8,128)(2,1)}), bf16[2816,1024]{1,0:T(8,128)(2,1)}) %all-gather.22.cloned.1.call-update) | async-done | bytes 5767184 | tf_op jit(solution)/shard_map/all_gather | solution.py:38
  404.5 7.1 multiply_convert_fusion.1
  414.5 9.2 multiply_reduce_fusion.4
  438.4 9.0 all_gather.66
  447.4 16.6 %all-gather.2 = bf16[1,256,1024]{2,1,0:T(8,128)(2,1)} all-gather(bf16[1,128,1024]{2,1,0:T(8,128)(2,1)} %param.33), channel_id=4, replica_groups=mesh['batch'=2,'seq'=16] {'batch'}, dimensions={1}, use_global_device_ids=true | all-gather | bytes 786432 | tf_op jit(solution)/shard_map/all_gather | solution.py:42
  464.0 14.8 %all_gather.70 = bf16[256,1024]{1,0:T(8,128)(2,1)} all-gather(bf16[128,1024]{1,0:T(8,128)(2,1)S(1)} %copy-done.18), channel_id=1, replica_groups=mesh['batch'=2,'seq'=16] {'batch'}, dimensions={0}, use_global_device_ids=true | all-gather | bytes 786432 | tf_op jit(solution)/shard_map/all_gather | solution.py:42
  478.9 14.6 %all_gather.68 = bf16[256,1024]{1,0:T(8,128)(2,1)S(1)} all-gather(bf16[128,1024]{1,0:T(8,128)(2,1)} %copy-done.32), channel_id=1, replica_groups=mesh['batch'=2,'seq'=16] {'batch'}, dimensions={0}, use_global_device_ids=true | all-gather | bytes 786432 | tf_op jit(solution)/shard_map/all_gather | solution.py:42
  493.4 10.4 %all_gather.69 = bf16[256,1024]{1,0:T(8,128)(2,1)S(1)} all-gather(bf16[128,1024]{1,0:T(8,128)(2,1)} %copy-done.23), channel_id=1, replica_groups=mesh['batch'=2,'seq'=16] {'batch'}, dimensions={0}, use_global_device_ids=true | all-gather | bytes 786432 | tf_op jit(solution)/shard_map/all_gather | solution.py:42
  509.8 3.8 convolution_convert_fusion.2
  513.6 6.1 convolution_convert_fusion
  519.7 35.4 %all-gather.24.cloned.1.call-done = bf16[16,4,128,256]{3,2,1,0:T(8,128)(2,1)} async-done(((bf16[1,4,128,256]{3,2,1,0:T(8,128)(2,1)}), bf16[16,4,128,256]{3,2,1,0:T(8,128)(2,1)}) %all-gather.24.cloned.1.call-update) | async-done | bytes 4194320 | tf_op jit(solution)/shard_map/all_gather | solution.py:241
  565.9 5.0 fusion.128
  572.8 24.4 %all-gather.26.cloned.1.call-done = bf16[256,3072]{1,0:T(8,128)(2,1)} async-done(((bf16[128,3072]{1,0:T(8,128)(2,1)}), bf16[256,3072]{1,0:T(8,128)(2,1)}) %all-gather.26.cloned.1.call-update) | async-done | bytes 1572880 | tf_op jit(solution)/shard_map/all_gather | solution.py:42
  597.3 4.1 convolution_convert_fusion.1
  602.5 4.3 fusion.3
  607.9 118.0 %all-reduce.5.cloned.1.call-done = f32[2,13696]{1,0:T(2,128)} async-done(((f32[2,13696]{1,0:T(2,128)}), f32[2,13696]{1,0:T(2,128)}) %all-reduce.5.cloned.1.call-update) | async-done | bytes 109584 | tf_op jit(solution)/shard_map/psum | solution.py:306
  733.0 237.3 %all-reduce.7.cloned.1.call-done = (bf16[512,3072]{1,0:T(8,128)(2,1)}, bf16[512,5632]{1,0:T(8,128)(2,1)}, bf16[1024,512]{1,0:T(8,128)(2,1)}, bf16[1408,1024]{1,0:T(8,128)(2,1)}) async-done(((bf16[512,3072]{1,0:T(8,128)(2,1)}, bf16[512,5632]{1,0:T(8,128)(2,1)}, bf16[1024,512]{1,0:T(8,128)(2,1)}, bf16[1408,1024]{1,0:T(8,128)(2,1)}), (bf16[512,3072]{1,0:T(8,128)(2,1)}, bf16[512,5632]{1,0:T(8,128)(2,1)}, ...) | async-done | bytes 12845072 | tf_op jit(solution)/shard_map/psum | solution.py:52
  977.4 5.2 fusion.132
  (345 shorter events, 100.1 us)
Async XLA Ops:
  7.2 86.5 %all-gather.14.cloned.1.call-start = ((), (), s32[]{:S(2)}) async-start(), calls=%async_computation | async-start | bytes 9437184 | tf_op jit(solution)/shard_map/all_gather | solution.py:38
  10.5 170.6 %all-gather.16.cloned.1.call-start = ((), (), s32[]{:S(2)}) async-start(), calls=%async_computation.1 | async-start | bytes 4456448 | tf_op jit(solution)/shard_map/all_gather | solution.py:166
  20.7 76.8 %copy-start.42 = (s32[2,64]{1,0:T(2,128)}, s32[2,64]{1,0:T(2,128)S(1)}, u32[]{:S(2)}) copy-start(s32[2,64]{1,0:T(2,128)S(1)} %eq.73) | copy-start | bytes 1540
  21.2 76.3 %copy-start.59 = (f32[128]{0:T(128)}, f32[128]{0:T(128)S(1)}, u32[]{:S(2)}) copy-start(f32[128]{0:T(128)S(1)} %add_rsqrt_fusion.2) | copy-start | bytes 1540
  21.4 76.1 %copy-start.45 = (f32[128,16]{0,1:T(8,128)}, f32[128,16]{0,1:T(8,128)S(1)}, u32[]{:S(2)}) copy-start(f32[128,16]{0,1:T(8,128)S(1)} %fusion.65) | copy-start | bytes 24580
  23.0 76.2 %copy-start.38 = (f32[2,4,1,128]{3,2,1,0:T(1,128)}, f32[2,4,1,128]{3,2,1,0:T(1,128)S(1)}, u32[]{:S(2)}) copy-start(f32[2,4,1,128]{3,2,1,0:T(1,128)S(1)} %slice.232) | copy-start | bytes 12292
  26.1 71.4 %copy-start.67 = (f32[2]{0:T(128)}, f32[2]{0:T(128)S(1)}, u32[]{:S(2)}) copy-start(f32[2]{0:T(128)S(1)} %slice_reduce_fusion.2) | copy-start | bytes 28
  26.2 73.0 %copy-start.56 = (f32[2,64]{1,0:T(2,128)}, f32[2,64]{1,0:T(2,128)S(1)}, u32[]{:S(2)}) copy-start(f32[2,64]{1,0:T(2,128)S(1)} %compare_convert_fusion) | copy-start | bytes 1540
  27.0 73.4 %copy-start.47 = (f32[4,128]{1,0:T(4,128)}, f32[4,128]{1,0:T(4,128)S(1)}, u32[]{:S(2)}) copy-start(f32[4,128]{1,0:T(4,128)S(1)} %get-tuple-element.120) | copy-start | bytes 6148
  98.8 80.3 %copy-start.7 = (f32[2,64,4,128]{3,2,1,0:T(4,128)}, f32[2,64,4,128]{3,2,1,0:T(4,128)S(1)}, u32[]{:S(2)}) copy-start(f32[2,64,4,128]{3,2,1,0:T(4,128)S(1)} %reshape.398) | copy-start | bytes 786436
  101.3 89.0 %all-gather.18.cloned.1.call-start = ((), (), s32[]{:S(2)}) async-start(), calls=%async_computation.2 | async-start | bytes 3145728 | tf_op jit(solution)/shard_map/all_gather | solution.py:38
  102.0 226.7 %all-gather.20.cloned.1.call-start = ((), (), s32[]{:S(2)}) async-start(), calls=%async_computation.3 | async-start | bytes 17301504 | tf_op jit(solution)/shard_map/all_gather | solution.py:38
  107.7 70.6 %copy-start.43 = (s32[2,64]{1,0:T(2,128)S(1)}, s32[2,64]{1,0:T(2,128)}, u32[]{:S(2)}) copy-start(s32[2,64]{1,0:T(2,128)} %copy-done.42) | copy-start | bytes 1540
  107.7 70.6 %copy-start.64 = (f32[2]{0:T(128)S(1)}, f32[2]{0:T(128)}, u32[]{:S(2)}) copy-start(f32[2]{0:T(128)} %copy-done.63) | copy-start | bytes 28
  107.7 296.8 %all-gather.22.cloned.1.call-start = ((), (), s32[]{:S(2)}) async-start(), calls=%async_computation.4 | async-start | bytes 8650752 | tf_op jit(solution)/shard_map/all_gather | solution.py:38
  108.3 401.5 %all-gather.30.cloned.1.call-start = ((), (), s32[]{:S(2)}) async-start(), calls=%async_computation.9 | async-start | bytes 2162688 | tf_op jit(solution)/shard_map/all_gather | solution.py:42
  193.6 231.0 %copy-start.61 = (f32[128]{0:T(128)}, f32[128]{0:T(128)S(1)}, u32[]{:S(2)}) copy-start(f32[128]{0:T(128)S(1)} %add_rsqrt_fusion.1) | copy-start | bytes 1540
  193.8 142.5 %copy-start.17 = (bf16[128,1024]{1,0:T(8,128)(2,1)}, bf16[128,1024]{1,0:T(8,128)(2,1)S(1)}, u32[]{:S(2)}) copy-start(bf16[128,1024]{1,0:T(8,128)(2,1)S(1)} %multiply_convert_fusion.4) | copy-start | bytes 786436
  193.8 210.8 %copy-start.24 = (bf16[1,128,1024]{2,1,0:T(8,128)(2,1)S(1)}, bf16[1,128,1024]{2,1,0:T(8,128)(2,1)}, u32[]{:S(2)}) copy-start(bf16[1,128,1024]{2,1,0:T(8,128)(2,1)} %param.33) | copy-start | bytes 786436
  411.6 102.0 %all-gather.28.cloned.1.call-start = ((), (), s32[]{:S(2)}) async-start(), calls=%async_computation.8 | async-start | bytes 4325376 | tf_op jit(solution)/shard_map/all_gather | solution.py:42
  414.2 140.9 %all-gather.24.cloned.1.call-start = ((), (), s32[]{:S(2)}) async-start(), calls=%async_computation.5 | async-start | bytes 4456448 | tf_op jit(solution)/shard_map/all_gather | solution.py:241
  437.5 159.7 %all-gather.26.cloned.1.call-start = ((), (), s32[]{:S(2)}) async-start(), calls=%async_computation.7 | async-start | bytes 2359296 | tf_op jit(solution)/shard_map/all_gather | solution.py:42
  571.4 154.5 %all-reduce.5.cloned.1.call-start = ((), (), s32[]{:S(2)}) async-start(), calls=%async_computation.6 | async-start | bytes 219136 | tf_op jit(solution)/shard_map/psum | solution.py:306
  572.5 397.8 %all-reduce.7.cloned.1.call-start = ((), (), s32[]{:S(2)}) async-start(), calls=%async_computation.10 | async-start | bytes 25690112 | tf_op jit(solution)/shard_map/psum | solution.py:52
  (66 other events, 636.0 us)
Sparse Core Ops, SparseCore 0:
  10.6 83.0 all-gather.13
  101.4 51.0 all-gather.15
  154.1 31.5 all-gather.17
  187.7 140.9 all-gather.19
  330.1 74.4 all-gather.21
  411.8 25.6 all-gather.29
  439.6 62.1 all-gather.27
  504.6 50.5 all-gather.23
  571.5 25.6 all-gather.25
  603.2 122.5 all-reduce.4
  731.6 238.6 all-reduce.6
